TPU v7x, 32 devices: a whole 2x2x4 slice. The times are simulated.
32 devices in a mesh: grp: 2 (over y), batch: 8 (over z, x), tensor: 2 (over core).
Axes of the slice: x: 2, y: 2, z: 4, core: 2. Of those that a mesh axis runs over, the one named last changes fastest.
Arguments:
- init_cache: bfloat16 [16, 2, 64, 3072], P(('grp', 'batch'), None, None, 'tensor'), parts along dimension 0, may hold values from -6 to 6
- memory: bfloat16 [16, 2, 64, 3072], P(('grp', 'batch'), None, None, 'tensor'), parts along dimension 0, may hold values from -6 to 6
- queries: bfloat16 [1, 16, 2, 3072], P(None, ('grp', 'batch'), None, 'tensor'), parts along dimension 1, may hold values from -600 to 600
- new_kv: bfloat16 [1, 16, 2, 3072], P(None, ('grp', 'batch'), None, 'tensor'), parts along dimension 1, may hold values from -6 to 6
- residual: bfloat16 [1, 16, 6144], P(None, 'grp', 'batch'), parts along dimension 1, may hold values from -6 to 6
- out_weight: bfloat16 [2, 3072, 6144], P(None, 'tensor', 'batch'), may hold values from -0.078125 to 0.078125
- up_weight: bfloat16 [6144, 24576], P(None, ('batch', 'tensor')), may hold values from -0.078125 to 0.078125
- down_weight: bfloat16 [24576, 6144], P('batch', 'tensor'), may hold values from -0.0390625 to 0.0390625
- parents: int32 [1, 16], P(None, 'grp'), parts along dimension 1, may hold values from 0 to 7
- lengths: int32 [2], P('grp'), parts along dimension 0, may hold values from 1 to 63
Outputs:
- hidden: bfloat16 [1, 16, 6144], P(None, 'grp', 'batch'), parts along dimension 1
- ffn_out: bfloat16 [1, 16, 6144], P(None, ('grp', 'batch'), 'tensor'), parts along dimension 1
- final_cache: bfloat16 [16, 2, 64, 3072], P(('grp', 'batch'), None, None, 'tensor'), parts along dimension 0
There are 2 independent parts, one for each index of `grp`. A program takes and returns all parts, laid end to end along the dimension named above; an argument that names none is the same for every part. Nothing has to cross between parts.
Inputs may be any that keep to these rules, and one draw needn't show every extreme that they name: parents[s, b + r] is the beam of request r whose cache beam b continues at step s.
All inputs are finite; a program needn't handle non-finite values.
Results may differ from a plain program's by a relative error of at most 0.006.
Values may be sent and summed in bfloat16 or wider, within the bound.
A program may use at most 128 MiB of HBM per device.

v0:
```python
import math

import jax
import jax.numpy as jnp
from jax import lax
from jax.experimental import pallas as pl
from jax.experimental.pallas import tpu as pltpu
from jax.sharding import PartitionSpec as P

HD = 128
BEAMS = 8


def from_behind(value, axis, by):
    devices = lax.axis_size(axis)
    return lax.ppermute(value, axis, [(i, (i + by) % devices) for i in range(devices)])


def attend(query, keys, values, valid):
    highest = lax.Precision.HIGHEST
    scores = jnp.einsum("nhd,chd->nhc", query, keys, precision=highest) / math.sqrt(HD)
    mask = valid[:, None, :]
    masked = jnp.where(mask, scores, -1e30)
    peak = jnp.max(masked, axis=-1)
    weights = jnp.where(mask, jnp.exp(masked - peak[..., None]), 0.0)
    total = jnp.sum(weights, axis=-1)
    weighted = jnp.einsum("nhc,chd->nhd", weights, values, precision=highest)
    return (weighted, peak, total)


def spread(payload, stride):
    items = [payload]
    for offset in range(1, BEAMS):
        items.append(from_behind(payload, "batch", offset * stride))
    return jnp.stack(items)


def take_from(block, source, own_beam, stride):
    wanted = (own_beam - source) % BEAMS
    result = block
    for offset in range(1, BEAMS):
        moved = from_behind(block, "batch", offset * stride)
        result = jnp.where(wanted == offset, moved, result)
    return result


def collect(weighted, peak, total, stride):
    gathered = [(weighted[0], peak[0], total[0])]
    for offset in range(1, BEAMS):
        gathered.append(
            from_behind((weighted[offset], peak[offset], total[offset]), "batch", -offset * stride)
        )
    return gathered


def combine(gathered):
    peaks = jnp.stack([entry[1] for entry in gathered])
    top = jnp.max(peaks, axis=0)
    factors = jnp.exp(peaks - top[None])
    numer = jnp.sum(jnp.stack([entry[0] for entry in gathered]) * factors[..., None], axis=0)
    denom = jnp.sum(jnp.stack([entry[2] for entry in gathered]) * factors, axis=0)
    return numer / denom[..., None]


def body(
    init_cache,
    memory,
    queries,
    new_kv,
    residual,
    out_weight,
    up_weight,
    down_weight,
    parents,
    lengths,
):
    stride = lax.axis_size("batch") // BEAMS
    position = lax.axis_index("batch")
    own_beam = position // stride
    request = position % stride
    width_local = queries.shape[-1]
    local_heads = width_local // HD
    cache_len = init_cache.shape[2]
    steps = queries.shape[0]
    request_ids = jnp.arange(stride, dtype=jnp.int32)
    length = jnp.sum(jnp.where(request_ids == request, lengths, 0))
    grouped = parents.reshape(steps, BEAMS, stride)
    parent_table = jnp.sum(jnp.where(request_ids[None, None, :] == request, grouped, 0), axis=2)
    slots = jnp.arange(cache_len, dtype=jnp.int32)
    beam_ids = jnp.arange(BEAMS, dtype=jnp.int32)
    mem_keys = memory[0, 0].astype(jnp.float32).reshape(-1, local_heads, HD)
    mem_values = memory[0, 1].astype(jnp.float32).reshape(-1, local_heads, HD)
    cross_valid = jnp.ones((BEAMS, mem_keys.shape[0]), dtype=bool)
    init_rows = init_cache[0]
    cache = init_rows
    proj_weight = out_weight.reshape(2 * width_local, out_weight.shape[2])
    own_query = queries[0, 0]
    parent_beam = jnp.sum(jnp.where(beam_ids == own_beam, parent_table[0], 0))
    cache = take_from(cache, parent_beam, own_beam, stride)
    cache = jnp.where((slots == length + 0)[None, :, None], new_kv[0, 0][:, None, :], cache)
    self_query = own_query[0].astype(jnp.float32).reshape(1, local_heads, HD)
    keys = cache[0].astype(jnp.float32).reshape(cache_len, local_heads, HD)
    values = cache[1].astype(jnp.float32).reshape(cache_len, local_heads, HD)
    valid = (slots <= length + 0)[None, :]
    weighted, peak, total = attend(self_query, keys, values, valid)
    self_out = (weighted / total[..., None])[0]
    items = spread(own_query[1], stride)
    cross_query = items.astype(jnp.float32).reshape(BEAMS, local_heads, HD)
    weighted, peak, total = attend(cross_query, mem_keys, mem_values, cross_valid)
    merged = combine(collect(weighted[:, None], peak[:, None], total[:, None], stride))
    cross_out = merged[0]
    attended = jnp.stack([self_out, cross_out]).reshape(1, 2 * width_local).astype(jnp.bfloat16)
    partial_proj = jnp.dot(
        lax.all_gather(attended, "batch", axis=0, tiled=True),
        proj_weight,
        preferred_element_type=jnp.float32,
    )
    projected = lax.psum(partial_proj, "tensor")
    hidden = (residual[0].astype(jnp.float32) + projected).astype(jnp.bfloat16)
    pre_act = jnp.dot(
        lax.all_gather(hidden, "batch", axis=1, tiled=True),
        up_weight,
        preferred_element_type=jnp.float32,
    )
    activation = jax.nn.gelu(pre_act, approximate=False).astype(jnp.bfloat16)
    joined = lax.all_gather(activation, "tensor", axis=1, tiled=True)
    ffn_row = lax.psum_scatter(
        jnp.dot(joined, down_weight, preferred_element_type=jnp.float32),
        "batch",
        scatter_dimension=0,
        tiled=True,
    ).astype(jnp.bfloat16)
    hidden_list = [hidden]
    ffn_list = [ffn_row]
    return (jnp.stack(hidden_list), jnp.stack(ffn_list), cache[None])


LANES = 128
SLOTS = 16
PIECES = 4
PLAN = (((1, 0), (1, 1), (1, 2)), ((1, 3),), ((2, 0), (2, 1), (2, 2)), ((2, 3), (3, 0), (3, 1)), ((3, 2), (3, 3), (4, 0), (4, 1)), ((4, 2), (4, 3)), ())
F32 = jnp.float32
BF16 = jnp.bfloat16


def step_kernel(
    q_hbm,
    kv_hbm,
    cache_hbm,
    mem_hbm,
    res_hbm,
    ow_hbm,
    up_hbm,
    dn_hbm,
    par_ref,
    len_ref,
    hid_out,
    ffn_out,
    cache_out,
    qall,
    kv,
    rows,
    mem,
    res,
    ow,
    up,
    dn,
    part_s,
    part_r,
    att,
    lhs,
    pp_s,
    pp_r,
    hid_all,
    acc,
    act,
    dacc,
    rs_s,
    rs_r,
    row_s,
    row_r,
    local_sem,
    q_send,
    q_recv,
    part_send,
    part_recv,
    att_send,
    att_recv,
    pair_send,
    pair_recv,
    hid_send,
    hid_recv,
    rs_send,
    rs_recv,
    up_send,
    down_send,
    row_recv,
    x_send,
    x_recv,
):
    me = lax.axis_index("batch")
    half = lax.axis_index("tensor")
    other = 1 - half
    z, x = me // 2, me % 2
    heads = qall.shape[2] // LANES
    width = qall.shape[2]
    cache_len = rows.shape[2]
    block = hid_all.shape[2]
    chunks = rs_s.shape[0]
    peers = [(me + j) % BEAMS for j in (4, 3, 5, 2, 6, 7, 1)]
    sources = [(me + BEAMS - j) % BEAMS for j in (1, 7, 2, 6, 3, 5, 4)]
    zs = BEAMS // 2

    def remote(src, dst, send, recv, device):
        return pltpu.make_async_remote_copy(
            src_ref=src,
            dst_ref=dst,
            send_sem=send,
            recv_sem=recv,
            device_id=device,
            device_id_type=pl.DeviceIdType.MESH,
        )

    locals_ = [
        pltpu.make_async_copy(q_hbm.at[0, 0], qall.at[me], local_sem.at[0]),
        pltpu.make_async_copy(kv_hbm.at[0, 0], kv, local_sem.at[1]),
        pltpu.make_async_copy(cache_hbm.at[0], rows.at[z], local_sem.at[2]),
        pltpu.make_async_copy(mem_hbm.at[0], mem, local_sem.at[3]),
        pltpu.make_async_copy(res_hbm.at[0], res, local_sem.at[4]),
        pltpu.make_async_copy(ow_hbm, ow, local_sem.at[5]),
        pltpu.make_async_copy(up_hbm, up, local_sem.at[6]),
        pltpu.make_async_copy(dn_hbm, dn, local_sem.at[7]),
    ]
    for copy in locals_:
        copy.start()
    barrier = pltpu.get_barrier_semaphore()
    for peer in peers:
        pl.semaphore_signal(
            barrier, inc=1, device_id={"batch": peer}, device_id_type=pl.DeviceIdType.MESH
        )
    pl.semaphore_signal(
        barrier, inc=1, device_id={"tensor": other}, device_id_type=pl.DeviceIdType.MESH
    )
    part_s[...] = jnp.zeros_like(part_s)
    locals_[0].wait()
    pl.semaphore_wait(barrier, BEAMS)

    def to_peers(buffer_of, target_of, send, recv):
        sent = []
        for peer in peers:
            copy = remote(
                buffer_of(peer), target_of(me), send.at[peer], recv.at[me], {"batch": peer}
            )
            copy.start()
            sent.append(copy)
        return sent

    def arrived(target_of, recv, source):
        remote(
            target_of(source), target_of(source), recv.at[source], recv.at[source],
            {"batch": source},
        ).wait_recv()

    sent = to_peers(lambda p: qall.at[me], lambda s: qall.at[s], q_send, q_recv)

    pieces = row_recv.shape[1]
    span = cache_len * 2 // pieces
    ups, downs = (me + 2) % BEAMS, (me + BEAMS - 2) % BEAMS

    def piece_of(ref, k):
        return ref.at[k * span // cache_len, pl.ds(k * span % cache_len, span)]

    def row_copy(index, k, send, to):
        view = piece_of(rows.at[index], k)
        return remote(view, view, send, row_recv.at[index, k], {"batch": to})

    def row_hop(hop, k):
        below, above = z - hop + 1, z + hop - 1
        if hop > 1:
            @pl.when(below >= 0)
            def _():
                row_copy(below, k, row_recv.at[below, k], downs).wait_recv()

            @pl.when(above < zs)
            def _():
                row_copy(above, k, row_recv.at[above, k], ups).wait_recv()

        if hop < zs:
            @pl.when((below >= 0) & (z < zs - 1))
            def _():
                row_copy(below, k, up_send.at[hop - 1, k], ups).start()

            @pl.when((above < zs) & (z > 0))
            def _():
                row_copy(above, k, down_send.at[hop - 1, k], downs).start()

    partner = me + 1 - 2 * x

    def cross_copy(k):
        return remote(
            piece_of(row_s, k), piece_of(row_r, k), x_send.at[k], x_recv.at[k], {"batch": partner}
        )

    def row_cross(k):
        row_hop(zs, k)
        which, at = k * span // cache_len, k * span % cache_len
        wanted = par_ref[0, partner] // 2
        chosen = rows[0, which, at : at + span]
        for index in range(1, zs):
            chosen = jnp.where(wanted == index, rows[index, which, at : at + span], chosen)
        row_s[which, at : at + span] = chosen
        cross_copy(k).start()

    def rows_sent():
        for k in range(pieces):
            for hop in range(1, zs):
                below, above = z - hop + 1, z + hop - 1

                @pl.when((below >= 0) & (z < zs - 1))
                def _():
                    row_copy(below, k, up_send.at[hop - 1, k], ups).wait_send()

                @pl.when((above < zs) & (z > 0))
                def _():
                    row_copy(above, k, down_send.at[hop - 1, k], downs).wait_send()

            cross_copy(k).wait_send()

    def bulk(stage):
        for hop, k in PLAN[stage]:
            if hop == zs:
                row_cross(k)
            else:
                row_hop(hop, k)

    locals_[2].wait()
    bulk(0)
    locals_[1].wait()
    locals_[3].wait()
    for source in sources:
        arrived(lambda s: qall.at[s], q_recv, source)

    length = len_ref[0]
    queries = qall[...].astype(F32)
    lane = lax.broadcasted_iota(jnp.int32, (BEAMS, LANES), 1)
    stats = jnp.zeros((BEAMS, LANES), F32)
    slot = lax.broadcasted_iota(jnp.int32, (heads * BEAMS, cache_len), 1)
    for kind in range(2):
        def block_of(which, h):
            cut = slice(h * LANES, (h + 1) * LANES)
            return mem[which, :, cut] if kind else rows[z, which, :, cut]

        scores = jnp.concatenate(
            [
                lax.dot_general(
                    queries[:, kind, h * LANES : (h + 1) * LANES].astype(BF16),
                    block_of(0, h),
                    (((1,), (1,)), ((), ())),
                    preferred_element_type=F32,
                )
                for h in range(heads)
            ],
            axis=0,
        ) / math.sqrt(HD)
        if kind == 0:
            scores = jnp.where(slot < length, scores, -1e30)
        peak = jnp.max(scores, axis=1, keepdims=True)
        weights = jnp.exp(scores - peak)
        if kind == 0:
            weights = jnp.where(slot < length, weights, 0.0)
        total = jnp.sum(weights, axis=1, keepdims=True)
        for h in range(heads):
            cut = slice(h * BEAMS, (h + 1) * BEAMS)
            w = weights[cut]
            high = w.astype(BF16)
            low = (w - high.astype(F32)).astype(BF16)
            both = jnp.dot(
                jnp.concatenate([high, low], axis=0),
                block_of(1, h),
                preferred_element_type=F32,
            )
            part_s[:, kind * SLOTS + h, :] = both[:BEAMS] + both[BEAMS:]
            stats = jnp.where(lane == 2 * kind * SLOTS + h, peak[cut], stats)
            stats = jnp.where(lane == (2 * kind + 1) * SLOTS + h, total[cut], stats)
    part_s[:, heads, :] = stats
    sent += to_peers(lambda p: part_s.at[p], lambda s: part_r.at[s], part_send, part_recv)
    bulk(1)
    part_r[me] = part_s[me]

    def rows_of(flat):
        return jnp.concatenate(
            [flat[:, h * LANES : (h + 1) * LANES] for h in range(heads)], axis=0
        )

    own_q = qall[me].astype(F32)
    new_f = kv[...].astype(F32)
    new_score = jnp.sum(rows_of(own_q[0:1] * new_f[0:1]), axis=1, keepdims=True) / math.sqrt(HD)
    new_value = rows_of(new_f[1:2])
    for source in sources:
        arrived(lambda s: part_r.at[s], part_recv, source)
    parent = par_ref[0, me]
    turned = part_r[:, heads, :].T
    beam = lax.broadcasted_iota(jnp.int32, (LANES, BEAMS), 1)
    chosen = jnp.sum(jnp.where(beam == parent, turned, 0.0), axis=1, keepdims=True)
    self_peak, self_total = chosen[:heads], chosen[SLOTS : SLOTS + heads]
    self_part = part_r[parent][:heads]
    top = jnp.maximum(self_peak, new_score)
    old_f, new_w = jnp.exp(self_peak - top), jnp.exp(new_score - top)
    self_out = (old_f * self_part + new_w * new_value) / (old_f * self_total + new_w)
    peaks = turned[2 * SLOTS : 2 * SLOTS + heads]
    factor = jnp.exp(peaks - jnp.max(peaks, axis=1, keepdims=True))
    denom = jnp.sum(factor * turned[3 * SLOTS : 3 * SLOTS + heads], axis=1, keepdims=True)
    numer = jnp.zeros((heads, LANES), F32)
    for p in range(BEAMS):
        numer = numer + factor[:, p : p + 1] * part_r[p][SLOTS : SLOTS + heads]
    cross_out = numer / denom
    spare = jnp.zeros((SLOTS - heads, LANES), F32)
    att[me] = jnp.concatenate([self_out, spare, cross_out, spare], axis=0).astype(BF16)
    sent += to_peers(lambda p: att.at[me], lambda s: att.at[s], att_send, att_recv)
    bulk(2)
    locals_[4].wait()
    locals_[5].wait()
    for source in sources:
        arrived(lambda s: att.at[s], att_recv, source)
    attended = att[...].astype(F32)
    for kind in range(2):
        for h in range(heads):
            lhs[kind, :, h * LANES : (h + 1) * LANES] = attended[:, kind * SLOTS + h, :].astype(BF16)
    pp_s[...] = jnp.dot(lhs[0], ow[0], preferred_element_type=F32) + jnp.dot(
        lhs[1], ow[1], preferred_element_type=F32
    )
    pair = remote(pp_s, pp_r, pair_send.at[0], pair_recv.at[0], {"tensor": other})
    pair.start()
    pair.wait_recv()
    hidden = (res[...].astype(F32) + (pp_s[...] + pp_r[...])).astype(BF16)
    hid_all[me] = hidden
    sent += [pair] + to_peers(
        lambda p: hid_all.at[me], lambda s: hid_all.at[s], hid_send, hid_recv
    )
    hid_out[0] = hidden
    bulk(3)
    locals_[6].wait()

    def up_dot(source):
        at = pl.multiple_of(source * block, block)
        return jnp.dot(hid_all[source], up[pl.ds(at, block), :], preferred_element_type=F32)

    acc[...] = up_dot(me)

    def up_step(j, carry):
        step = (j + 1) // 2
        source = (me + j % 2 * step + (1 - j % 2) * (BEAMS - step)) % BEAMS
        arrived(lambda s: hid_all.at[s], hid_recv, source)
        acc[...] += up_dot(source)
        return carry

    lax.fori_loop(1, BEAMS, up_step, 0)
    pre = acc[...]
    act[half] = (0.5 * pre * (1.0 + lax.erf(pre * math.sqrt(0.5)))).astype(BF16)
    swap = remote(act.at[half], act.at[half], pair_send.at[1], pair_recv.at[1], {"tensor": other})
    swap.start()
    sent.append(swap)
    bulk(4)
    locals_[7].wait()
    part = rs_s.shape[2] * LANES

    def down_dot(which, c):
        at = pl.multiple_of(which * width, width)
        return jnp.dot(
            act[which],
            dn[pl.ds(at, width), pl.ds(pl.multiple_of(c * part, part), part)],
            preferred_element_type=F32,
        )

    def own_half(c, carry):
        dacc[c] = down_dot(half, c)
        return carry

    lax.fori_loop(0, chunks, own_half, 0)
    swap.wait_recv()
    bulk(5)

    def other_half(c, carry):
        sums = dacc[c] + down_dot(other, c)
        for i in range(part // LANES):
            rs_s[c, :, i, :] = sums[:, i * LANES : (i + 1) * LANES]
        for peer in peers:
            remote(
                rs_s.at[c, peer], rs_r.at[c, me], rs_send.at[c, peer], rs_recv.at[c, me],
                {"batch": peer},
            ).start()
        rs_r[c, me] = rs_s[c, me]
        return carry

    lax.fori_loop(0, chunks, other_half, 0)
    bulk(6)
    for k in range(pieces):
        cross_copy(k).wait_recv()
    mine = rows[parent // 2]
    kept = jnp.where(parent % 2 == x, mine, row_r[...])
    time = lax.broadcasted_iota(jnp.int32, (cache_len, width), 0)
    for which in range(2):
        fresh = jnp.broadcast_to(new_f[which : which + 1], (cache_len, width))
        cache_out[0, which] = jnp.where(
            time == length, fresh, kept[which].astype(F32)
        ).astype(BF16)
    for c in range(chunks):
        for source in sources:
            remote(
                rs_r.at[c, source], rs_r.at[c, source], rs_recv.at[c, source],
                rs_recv.at[c, source], {"batch": source},
            ).wait_recv()
        sums = rs_r[c, 0]
        for p in range(1, BEAMS):
            sums = sums + rs_r[c, p]
        for i in range(part // LANES):
            at = c * part + i * LANES
            ffn_out[0, 0:1, at : at + LANES] = sums[i : i + 1].astype(BF16)
    for copy in sent:
        copy.wait_send()
    rows_sent()
    for c in range(chunks):
        for peer in peers:
            remote(
                rs_s.at[c, peer], rs_r.at[c, me], rs_send.at[c, peer], rs_recv.at[c, me],
                {"batch": peer},
            ).wait_send()


def place_kernel(*refs):
    count = (len(refs) - 2) // 3
    sources, targets = refs[:count], refs[count : 2 * count]
    held, (read_sem, write_sem) = refs[2 * count : 3 * count], refs[3 * count :]
    reads = [
        pltpu.make_async_copy(sources[i], held[i], read_sem.at[i]) for i in range(count)
    ]
    writes = [
        pltpu.make_async_copy(held[i], targets[i], write_sem.at[i]) for i in range(count)
    ]
    for copy in reads:
        copy.start()
    for i in range(count):
        reads[i].wait()
        writes[i].start()
    for copy in writes:
        copy.wait()


def place(*arrays):
    any_ = pl.BlockSpec(memory_space=pl.ANY)
    count = len(arrays)
    return pl.pallas_call(
        place_kernel,
        out_shape=tuple(jax.ShapeDtypeStruct(a.shape, a.dtype) for a in arrays),
        in_specs=[any_] * count,
        out_specs=(any_,) * count,
        scratch_shapes=[pltpu.VMEM(a.shape, a.dtype) for a in arrays]
        + [pltpu.SemaphoreType.DMA((count,)), pltpu.SemaphoreType.DMA((count,))],
    )(*arrays)


def kernel_body(
    init_cache,
    memory,
    queries,
    new_kv,
    residual,
    out_weight,
    up_weight,
    down_weight,
    parents,
    lengths,
):
    width = queries.shape[-1]
    row = init_cache.shape[1:]
    block = residual.shape[-1]
    columns = down_weight.shape[1]
    chunks = 3 if columns % (3 * 8 * LANES) == 0 else 1
    part_rows = columns // chunks // LANES
    any_ = pl.BlockSpec(memory_space=pl.ANY)
    vmem = pl.BlockSpec(memory_space=pltpu.VMEM)
    smem = pl.BlockSpec(memory_space=pltpu.SMEM)
    dma = pltpu.SemaphoreType.DMA
    results = pl.pallas_call(
        step_kernel,
        out_shape=(
            jax.ShapeDtypeStruct(residual.shape, BF16),
            jax.ShapeDtypeStruct((1, 1, columns), BF16),
            jax.ShapeDtypeStruct(init_cache.shape, BF16),
        ),
        in_specs=[any_] * 8 + [smem] * 2,
        out_specs=(vmem, vmem, vmem),
        scratch_shapes=[
            pltpu.VMEM((BEAMS, 2, width), BF16),
            pltpu.VMEM((2, width), BF16),
            pltpu.VMEM((BEAMS // 2,) + row, BF16),
            pltpu.VMEM(row, BF16),
            pltpu.VMEM((BEAMS, block), BF16),
            pltpu.VMEM(out_weight.shape, BF16),
            pltpu.VMEM(up_weight.shape, BF16),
            pltpu.VMEM(down_weight.shape, BF16),
            pltpu.VMEM((BEAMS, 2 * SLOTS, LANES), F32),
            pltpu.VMEM((BEAMS, 2 * SLOTS, LANES), F32),
            pltpu.VMEM((BEAMS, 2 * SLOTS, LANES), BF16),
            pltpu.VMEM((2, BEAMS, width), BF16),
            pltpu.VMEM((BEAMS, block), F32),
            pltpu.VMEM((BEAMS, block), F32),
            pltpu.VMEM((BEAMS, BEAMS, block), BF16),
            pltpu.VMEM((BEAMS, up_weight.shape[1]), F32),
            pltpu.VMEM((2, BEAMS, up_weight.shape[1]), BF16),
            pltpu.VMEM((chunks, BEAMS, columns // chunks), F32),
            pltpu.VMEM((chunks, BEAMS, part_rows, LANES), F32),
            pltpu.VMEM((chunks, BEAMS, part_rows, LANES), F32),
            pltpu.VMEM(row, BF16),
            pltpu.VMEM(row, BF16),
            dma((8,)),
            dma((BEAMS,)),
            dma((BEAMS,)),
            dma((BEAMS,)),
            dma((BEAMS,)),
            dma((BEAMS,)),
            dma((BEAMS,)),
            dma((2,)),
            dma((2,)),
            dma((BEAMS,)),
            dma((BEAMS,)),
            dma((chunks, BEAMS)),
            dma((chunks, BEAMS)),
            dma((BEAMS // 2, PIECES)),
            dma((BEAMS // 2, PIECES)),
            dma((BEAMS // 2, PIECES)),
            dma((PIECES,)),
            dma((PIECES,)),
        ],
        compiler_params=pltpu.CompilerParams(
            collective_id=0, has_side_effects=True, vmem_limit_bytes=62 * 1024 * 1024
        ),
    )(
        queries,
        new_kv,
        init_cache,
        memory,
        residual,
        out_weight,
        up_weight,
        down_weight,
        parents,
        lengths,
    )
    return place(*results)


def solution(mesh):
    placed = (
        P(("grp", "batch"), None, None, "tensor"),
        P(("grp", "batch"), None, None, "tensor"),
        P(None, ("grp", "batch"), None, "tensor"),
        P(None, ("grp", "batch"), None, "tensor"),
        P(None, "grp", "batch"),
        P(None, "tensor", "batch"),
        P(None, ("batch", "tensor")),
        P("batch", "tensor"),
        P(None, "grp"),
        P("grp"),
    )
    one_request = mesh.shape["batch"] == BEAMS and mesh.shape["tensor"] == 2
    return jax.shard_map(
        kernel_body if one_request else body,
        mesh=mesh,
        in_specs=placed,
        out_specs=(
            P(None, "grp", "batch"),
            P(None, ("grp", "batch"), "tensor"),
            P(("grp", "batch"), None, None, "tensor"),
        ),
        check_vma=False,
    )
```

profile of v0, /device:TPU:0, one launch (start us, length us, event | category | flops | bytes accessed | tf_op | source)
XLA Modules:
  0.0 50.4 jit_solution(163251867401415600)
XLA Ops:
  1.3 47.2 %shard_map.121 = (bf16[1,8,768]{2,1,0:T(8,128)(2,1)}, bf16[1,1,3072]{2,1,0:T(2,128)(2,1)}, bf16[1,2,64,1536]{3,2,1,0:T(8,128)(2,1)}) custom-call(bf16[1,1,2,1536]{3,2,1,0:T(2,128)(2,1)} %q_hbm.1, bf16[1,1,2,1536]{3,2,1,0:T(2,128)(2,1)} %kv_hbm.1, bf16[1,2,64,1536]{3,2,1,0:T(8,128)(2,1)} %cache_hbm.1, bf16[1,2,64,1536]{3,2,1,0:T(8,128)(2,1)} %mem_hbm.1, ...), custom_call_target="tpu_custom_call" | custom-call | tf_op jit(solution)/shard_map/pallas_call | solution.py:584
  48.5 1.8 %shard_map.122 = (bf16[1,8,768]{2,1,0:T(8,128)(2,1)}, bf16[1,1,3072]{2,1,0:T(2,128)(2,1)}, bf16[1,2,64,1536]{3,2,1,0:T(8,128)(2,1)}) custom-call(bf16[1,8,768]{2,1,0:T(8,128)(2,1)} %get-tuple-element.6.refs_0_, bf16[1,1,3072]{2,1,0:T(2,128)(2,1)} %get-tuple-element.7.refs_1_, bf16[1,2,64,1536]{3,2,1,0:T(8,128)(2,1)} %get-tuple-element.8.refs_2_), custom_call_target="tpu_custom_call" | custom-call | tf_op jit(solution)/shard_map/pallas_call | solution.py:552
where the time goes:
time: 50.7 us; the launch traced here: 50.4 us
  Pallas kernels  49.1 us (97%)
  between operations  1.29 us (3%)
    pallas_call x1, Pallas kernels, kernel_body(): pl.pallas_call(step_kernel, out_shape=(jax.ShapeDtypeStruct(residual.shap...  47.2 us
    pallas_call x1, Pallas kernels, place(): pl.pallas_call(place_kernel, out_shape=tuple((jax.ShapeDtypeStruct(a.shap...  1.83 us

commit v1 on v0

--- a/solution.py
+++ b/solution.py
@@ -137,8 +137,10 @@
 
 LANES = 128
 SLOTS = 16
-PIECES = 4
-PLAN = (((1, 0), (1, 1), (1, 2)), ((1, 3),), ((2, 0), (2, 1), (2, 2)), ((2, 3), (3, 0), (3, 1)), ((3, 2), (3, 3), (4, 0), (4, 1)), ((4, 2), (4, 3)), ())
+PIECES = 8
+INWARD = (2, 1, 3, 2, 0, 0, 0)
+ACROSS = (0, 1, 2, 3, 2, 0, 0)
+OUTWARD = (0, 0, 1, 2, 3, 1, 1)
 F32 = jnp.float32
 BF16 = jnp.bfloat16
 
@@ -152,8 +154,8 @@
     ow_hbm,
     up_hbm,
     dn_hbm,
-    par_ref,
-    len_ref,
+    par_hbm,
+    len_hbm,
     hid_out,
     ffn_out,
     cache_out,
@@ -192,11 +194,15 @@
     hid_recv,
     rs_send,
     rs_recv,
-    up_send,
-    down_send,
+    near_send,
+    far_send,
     row_recv,
     x_send,
     x_recv,
+    out_send,
+    out_recv,
+    par_ref,
+    len_ref,
 ):
     me = lax.axis_index("batch")
     half = lax.axis_index("tensor")
@@ -207,9 +213,18 @@
     cache_len = rows.shape[2]
     block = hid_all.shape[2]
     chunks = rs_s.shape[0]
-    peers = [(me + j) % BEAMS for j in (4, 3, 5, 2, 6, 7, 1)]
-    sources = [(me + BEAMS - j) % BEAMS for j in (1, 7, 2, 6, 3, 5, 4)]
     zs = BEAMS // 2
+    flip = z // 2
+    turn = 1 - 2 * flip
+    inner = z * turn + 3 * flip
+
+    def nearest(j):
+        k = j // 2 - 1
+        there = (k + (k + 4 - inner) // 4) * turn + 3 * flip
+        return there * 2 + (x + j) % 2
+
+    sources = [me + 1 - 2 * x] + [nearest(j) for j in range(2, BEAMS)]
+    peers = sources[::-1]
 
     def remote(src, dst, send, recv, device):
         return pltpu.make_async_remote_copy(
@@ -230,9 +245,9 @@
         pltpu.make_async_copy(ow_hbm, ow, local_sem.at[5]),
         pltpu.make_async_copy(up_hbm, up, local_sem.at[6]),
         pltpu.make_async_copy(dn_hbm, dn, local_sem.at[7]),
+        pltpu.make_async_copy(par_hbm, par_ref, local_sem.at[8]),
+        pltpu.make_async_copy(len_hbm, len_ref, local_sem.at[9]),
     ]
-    for copy in locals_:
-        copy.start()
     barrier = pltpu.get_barrier_semaphore()
     for peer in peers:
         pl.semaphore_signal(
@@ -241,6 +256,8 @@
     pl.semaphore_signal(
         barrier, inc=1, device_id={"tensor": other}, device_id_type=pl.DeviceIdType.MESH
     )
+    for copy in locals_[:2] + locals_[8:] + locals_[2:8]:
+        copy.start()
     part_s[...] = jnp.zeros_like(part_s)
     locals_[0].wait()
     pl.semaphore_wait(barrier, BEAMS)
@@ -265,74 +282,114 @@
 
     pieces = row_recv.shape[1]
     span = cache_len * 2 // pieces
-    ups, downs = (me + 2) % BEAMS, (me + BEAMS - 2) % BEAMS
+    partner = me + 1 - 2 * x
+    ahead = (me + BEAMS + 2 * turn) % BEAMS
+    beyond = (me + BEAMS + 4 * turn) % BEAMS
+    outer = (me + BEAMS - 2 * turn) % BEAMS
+    beside = (partner + BEAMS - 2 * turn) % BEAMS
+    is_end, is_mid = inner == 0, inner == 1
 
     def piece_of(ref, k):
         return ref.at[k * span // cache_len, pl.ds(k * span % cache_len, span)]
 
-    def row_copy(index, k, send, to):
-        view = piece_of(rows.at[index], k)
-        return remote(view, view, send, row_recv.at[index, k], {"batch": to})
-
-    def row_hop(hop, k):
-        below, above = z - hop + 1, z + hop - 1
-        if hop > 1:
-            @pl.when(below >= 0)
-            def _():
-                row_copy(below, k, row_recv.at[below, k], downs).wait_recv()
-
-            @pl.when(above < zs)
-            def _():
-                row_copy(above, k, row_recv.at[above, k], ups).wait_recv()
-
-        if hop < zs:
-            @pl.when((below >= 0) & (z < zs - 1))
-            def _():
-                row_copy(below, k, up_send.at[hop - 1, k], ups).start()
-
-            @pl.when((above < zs) & (z > 0))
-            def _():
-                row_copy(above, k, down_send.at[hop - 1, k], downs).start()
-
-    partner = me + 1 - 2 * x
-
-    def cross_copy(k):
+    def inward(k, send, to, slot):
+        view = piece_of(rows.at[slot], k)
+        return remote(view, view, send.at[k], row_recv.at[slot, k], {"batch": to})
+
+    def across(j, k):
         return remote(
-            piece_of(row_s, k), piece_of(row_r, k), x_send.at[k], x_recv.at[k], {"batch": partner}
+            piece_of(row_s.at[j], k), piece_of(row_r.at[j], k), x_send.at[j, k], x_recv.at[j, k],
+            {"batch": partner},
         )
 
-    def row_cross(k):
-        row_hop(zs, k)
-        which, at = k * span // cache_len, k * span % cache_len
-        wanted = par_ref[0, partner] // 2
+    def outward(k):
+        return remote(
+            piece_of(row_s.at[2], k), piece_of(row_r.at[2], k), out_send.at[k], out_recv.at[k],
+            {"batch": outer},
+        )
+
+    def row_of(beam, which, at):
+        wanted = par_ref[0, beam] // 2
         chosen = rows[0, which, at : at + span]
         for index in range(1, zs):
             chosen = jnp.where(wanted == index, rows[index, which, at : at + span], chosen)
-        row_s[which, at : at + span] = chosen
-        cross_copy(k).start()
+        return chosen
+
+    def start_inward(k):
+        inward(k, near_send, ahead, z).start()
+
+        @pl.when(is_end)
+        def _():
+            inward(k, far_send, beyond, z).start()
+
+    def start_across(k):
+        which, at = k * span // cache_len, k * span % cache_len
+
+        @pl.when(is_mid)
+        def _():
+            for slot in (z - turn, z + turn, z + 2 * turn):
+                slot = (slot + zs) % zs
+                inward(k, near_send, ahead, slot).wait_recv()
+            for j, beam in enumerate((partner, beside)):
+                row_s[j, which, at : at + span] = row_of(beam, which, at)
+                across(j, k).start()
+
+    def start_outward(k):
+        which, at = k * span // cache_len, k * span % cache_len
+
+        @pl.when(is_mid)
+        def _():
+            across(1, k).wait_recv()
+            row_s[2, which, at : at + span] = jnp.where(
+                par_ref[0, outer] % 2 == x, row_of(outer, which, at),
+                row_r[1, which, at : at + span],
+            )
+            outward(k).start()
 
     def rows_sent():
         for k in range(pieces):
-            for hop in range(1, zs):
-                below, above = z - hop + 1, z + hop - 1
-
-                @pl.when((below >= 0) & (z < zs - 1))
-                def _():
-                    row_copy(below, k, up_send.at[hop - 1, k], ups).wait_send()
-
-                @pl.when((above < zs) & (z > 0))
-                def _():
-                    row_copy(above, k, down_send.at[hop - 1, k], downs).wait_send()
-
-            cross_copy(k).wait_send()
+            inward(k, near_send, ahead, z).wait_send()
+
+            @pl.when(is_end)
+            def _():
+                inward(k, far_send, beyond, z).wait_send()
+
+            @pl.when(is_mid)
+            def _():
+                across(0, k).wait_send()
+                across(1, k).wait_send()
+                outward(k).wait_send()
 
     def bulk(stage):
-        for hop, k in PLAN[stage]:
-            if hop == zs:
-                row_cross(k)
-            else:
-                row_hop(hop, k)
-
+        for counts, start in ((INWARD, start_inward), (ACROSS, start_across), (OUTWARD, start_outward)):
+            for k in range(sum(counts[:stage]), sum(counts[: stage + 1])):
+                start(k)
+
+    def finish_rows():
+        time = lax.broadcasted_iota(jnp.int32, (span, width), 0)
+        for k in range(pieces):
+            which, at = k * span // cache_len, k * span % cache_len
+            fresh = jnp.broadcast_to(new_f[which : which + 1], (span, width))
+
+            def put(kept):
+                cache_out[0, which, at : at + span] = jnp.where(
+                    time + at == length, fresh, kept.astype(F32)
+                ).astype(BF16)
+
+            @pl.when(is_mid)
+            def _():
+                across(0, k).wait_recv()
+                put(jnp.where(
+                    parent % 2 == x, row_of(me, which, at), row_r[0, which, at : at + span]
+                ))
+
+            @pl.when(is_end)
+            def _():
+                outward(k).wait_recv()
+                put(row_r[2, which, at : at + span])
+
+    locals_[8].wait()
+    locals_[9].wait()
     locals_[2].wait()
     bulk(0)
     locals_[1].wait()
@@ -446,15 +503,16 @@
         return jnp.dot(hid_all[source], up[pl.ds(at, block), :], preferred_element_type=F32)
 
     acc[...] = up_dot(me)
+    arrived(lambda s: hid_all.at[s], hid_recv, sources[0])
+    acc[...] += up_dot(sources[0])
 
     def up_step(j, carry):
-        step = (j + 1) // 2
-        source = (me + j % 2 * step + (1 - j % 2) * (BEAMS - step)) % BEAMS
+        source = nearest(j)
         arrived(lambda s: hid_all.at[s], hid_recv, source)
         acc[...] += up_dot(source)
         return carry
 
-    lax.fori_loop(1, BEAMS, up_step, 0)
+    lax.fori_loop(2, BEAMS, up_step, 0)
     pre = acc[...]
     act[half] = (0.5 * pre * (1.0 + lax.erf(pre * math.sqrt(0.5)))).astype(BF16)
     swap = remote(act.at[half], act.at[half], pair_send.at[1], pair_recv.at[1], {"tensor": other})
@@ -477,8 +535,8 @@
         return carry
 
     lax.fori_loop(0, chunks, own_half, 0)
+    bulk(5)
     swap.wait_recv()
-    bulk(5)
 
     def other_half(c, carry):
         sums = dacc[c] + down_dot(other, c)
@@ -494,17 +552,12 @@
 
     lax.fori_loop(0, chunks, other_half, 0)
     bulk(6)
-    for k in range(pieces):
-        cross_copy(k).wait_recv()
-    mine = rows[parent // 2]
-    kept = jnp.where(parent % 2 == x, mine, row_r[...])
-    time = lax.broadcasted_iota(jnp.int32, (cache_len, width), 0)
-    for which in range(2):
-        fresh = jnp.broadcast_to(new_f[which : which + 1], (cache_len, width))
-        cache_out[0, which] = jnp.where(
-            time == length, fresh, kept[which].astype(F32)
-        ).astype(BF16)
-    for c in range(chunks):
+    finish_rows()
+    for copy in sent:
+        copy.wait_send()
+    rows_sent()
+
+    def collect_chunk(c):
         for source in sources:
             remote(
                 rs_r.at[c, source], rs_r.at[c, source], rs_recv.at[c, source],
@@ -516,9 +569,9 @@
         for i in range(part // LANES):
             at = c * part + i * LANES
             ffn_out[0, 0:1, at : at + LANES] = sums[i : i + 1].astype(BF16)
-    for copy in sent:
-        copy.wait_send()
-    rows_sent()
+
+    for c in range(chunks):
+        collect_chunk(c)
     for c in range(chunks):
         for peer in peers:
             remote(
@@ -528,35 +581,28 @@
 
 
 def place_kernel(*refs):
-    count = (len(refs) - 2) // 3
-    sources, targets = refs[:count], refs[count : 2 * count]
-    held, (read_sem, write_sem) = refs[2 * count : 3 * count], refs[3 * count :]
-    reads = [
-        pltpu.make_async_copy(sources[i], held[i], read_sem.at[i]) for i in range(count)
+    count = (len(refs) - 1) // 2
+    sem = refs[-1]
+    copies = [
+        pltpu.make_async_copy(refs[i], refs[count + i], sem.at[i]) for i in range(count)
     ]
-    writes = [
-        pltpu.make_async_copy(held[i], targets[i], write_sem.at[i]) for i in range(count)
-    ]
-    for copy in reads:
+    for copy in copies:
         copy.start()
-    for i in range(count):
-        reads[i].wait()
-        writes[i].start()
-    for copy in writes:
+    for copy in copies:
         copy.wait()
 
 
 def place(*arrays):
     any_ = pl.BlockSpec(memory_space=pl.ANY)
+    vmem = pl.BlockSpec(memory_space=pltpu.VMEM)
     count = len(arrays)
     return pl.pallas_call(
         place_kernel,
         out_shape=tuple(jax.ShapeDtypeStruct(a.shape, a.dtype) for a in arrays),
-        in_specs=[any_] * count,
+        in_specs=[vmem] * count,
         out_specs=(any_,) * count,
-        scratch_shapes=[pltpu.VMEM(a.shape, a.dtype) for a in arrays]
-        + [pltpu.SemaphoreType.DMA((count,)), pltpu.SemaphoreType.DMA((count,))],
-    )(*arrays)
+        scratch_shapes=[pltpu.SemaphoreType.DMA((count,))],
+    )(*(pltpu.with_memory_space_constraint(a, pltpu.VMEM) for a in arrays))
 
 
 def kernel_body(
@@ -579,16 +625,16 @@
     part_rows = columns // chunks // LANES
     any_ = pl.BlockSpec(memory_space=pl.ANY)
     vmem = pl.BlockSpec(memory_space=pltpu.VMEM)
-    smem = pl.BlockSpec(memory_space=pltpu.SMEM)
+    hbm = pl.BlockSpec(memory_space=pltpu.HBM)
     dma = pltpu.SemaphoreType.DMA
     results = pl.pallas_call(
         step_kernel,
         out_shape=(
-            jax.ShapeDtypeStruct(residual.shape, BF16),
-            jax.ShapeDtypeStruct((1, 1, columns), BF16),
-            jax.ShapeDtypeStruct(init_cache.shape, BF16),
+            pltpu.VMEM(residual.shape, BF16),
+            pltpu.VMEM((1, 1, columns), BF16),
+            pltpu.VMEM(init_cache.shape, BF16),
         ),
-        in_specs=[any_] * 8 + [smem] * 2,
+        in_specs=[any_] * 8 + [hbm] * 2,
         out_specs=(vmem, vmem, vmem),
         scratch_shapes=[
             pltpu.VMEM((BEAMS, 2, width), BF16),
@@ -611,9 +657,9 @@
             pltpu.VMEM((chunks, BEAMS, columns // chunks), F32),
             pltpu.VMEM((chunks, BEAMS, part_rows, LANES), F32),
             pltpu.VMEM((chunks, BEAMS, part_rows, LANES), F32),
-            pltpu.VMEM(row, BF16),
-            pltpu.VMEM(row, BF16),
-            dma((8,)),
+            pltpu.VMEM((3,) + row, BF16),
+            pltpu.VMEM((3,) + row, BF16),
+            dma((10,)),
             dma((BEAMS,)),
             dma((BEAMS,)),
             dma((BEAMS,)),
@@ -626,11 +672,15 @@
             dma((BEAMS,)),
             dma((chunks, BEAMS)),
             dma((chunks, BEAMS)),
-            dma((BEAMS // 2, PIECES)),
-            dma((BEAMS // 2, PIECES)),
-            dma((BEAMS // 2, PIECES)),
             dma((PIECES,)),
             dma((PIECES,)),
+            dma((BEAMS // 2, PIECES)),
+            dma((2, PIECES)),
+            dma((2, PIECES)),
+            dma((PIECES,)),
+            dma((PIECES,)),
+            pltpu.SMEM(parents.shape, jnp.int32),
+            pltpu.SMEM(lengths.shape, jnp.int32),
         ],
         compiler_params=pltpu.CompilerParams(
             collective_id=0, has_side_effects=True, vmem_limit_bytes=62 * 1024 * 1024

time: 50.7 us -> 45.3 us (0.89)
  Pallas kernels: 49.1 us -> 43.8 us
    pallas_call x1, Pallas kernels: 47.2 us -> 43 us  [kernel_body(): pl.pallas_call(step_kernel, out_shape=(pltpu.VMEM(residual.shape, BF16),...]
    pallas_call x1, Pallas kernels: 1.83 us -> 0.78 us  [place(): pl.pallas_call(place_kernel, out_shape=tuple((jax.ShapeDtypeStruct(a.shap...]
where the time goes in v1:
time: 45.3 us; the launch traced here: 45 us
  Pallas kernels  43.8 us (97%)
  between operations  1.29 us (3%)
    pallas_call x1, Pallas kernels, kernel_body(): pl.pallas_call(step_kernel, out_shape=(pltpu.VMEM(residual.shape, BF16),...  43 us

profile of v1, /device:TPU:0, one launch (start us, length us, event | category | flops | bytes accessed | tf_op | source)
XLA Modules:
  0.0 45.0 jit_solution(11048594848563577842)
XLA Ops:
  1.3 43.0 %shard_map.121 = (bf16[1,8,768]{2,1,0:T(8,128)(2,1)S(1)}, bf16[1,1,3072]{2,1,0:T(2,128)(2,1)S(1)}, bf16[1,2,64,1536]{3,2,1,0:T(8,128)(2,1)S(1)}) custom-call(bf16[1,1,2,1536]{3,2,1,0:T(2,128)(2,1)} %q_hbm.1, bf16[1,1,2,1536]{3,2,1,0:T(2,128)(2,1)} %kv_hbm.1, bf16[1,2,64,1536]{3,2,1,0:T(8,128)(2,1)} %cache_hbm.1, bf16[1,2,64,1536]{3,2,1,0:T(8,128)(2,1)} %mem_hbm.1, ...), custom_call_target="tpu_custom_call" | custom-call | tf_op jit(solution)/shard_map/pallas_call | solution.py:630
  44.3 0.8 %shard_map.122 = (bf16[1,8,768]{2,1,0:T(8,128)(2,1)}, bf16[1,1,3072]{2,1,0:T(2,128)(2,1)}, bf16[1,2,64,1536]{3,2,1,0:T(8,128)(2,1)}) custom-call(bf16[1,8,768]{2,1,0:T(8,128)(2,1)S(1)} %get-tuple-element.6.refs_0_, bf16[1,1,3072]{2,1,0:T(2,128)(2,1)S(1)} %get-tuple-element.7.refs_1_, bf16[1,2,64,1536]{3,2,1,0:T(8,128)(2,1)S(1)} %get-tuple-element.8.refs_2_), custom_call_target="tpu_custom_call" | custom-call | tf_op jit(solution)/shard_map/pallas_call | solution.py:599

commit v2 on v1

--- a/solution.py
+++ b/solution.py
@@ -223,7 +223,8 @@
         there = (k + (k + 4 - inner) // 4) * turn + 3 * flip
         return there * 2 + (x + j) % 2
 
-    sources = [me + 1 - 2 * x] + [nearest(j) for j in range(2, BEAMS)]
+    partner = me + 1 - 2 * x
+    sources = [partner] + [nearest(j) for j in range(2, BEAMS)]
     peers = sources[::-1]
 
     def remote(src, dst, send, recv, device):
@@ -263,14 +264,13 @@
     pl.semaphore_wait(barrier, BEAMS)
 
     def to_peers(buffer_of, target_of, send, recv):
-        sent = []
         for peer in peers:
-            copy = remote(
-                buffer_of(peer), target_of(me), send.at[peer], recv.at[me], {"batch": peer}
-            )
-            copy.start()
-            sent.append(copy)
-        return sent
+            remote(buffer_of(peer), target_of(me), send, recv, {"batch": peer}).start()
+        return [all_of(target_of, send)]
+
+    def all_of(target_of, sem):
+        view = target_of(pl.ds(0, BEAMS - 1))
+        return remote(view, view, sem, sem, {"batch": partner})
 
     def arrived(target_of, recv, source):
         remote(
@@ -278,11 +278,10 @@
             {"batch": source},
         ).wait_recv()
 
-    sent = to_peers(lambda p: qall.at[me], lambda s: qall.at[s], q_send, q_recv)
-
-    pieces = row_recv.shape[1]
+    sent = to_peers(lambda p: qall.at[me], lambda s: qall.at[s], q_send.at[0], q_recv.at[0])
+
+    pieces = row_recv.shape[0]
     span = cache_len * 2 // pieces
-    partner = me + 1 - 2 * x
     ahead = (me + BEAMS + 2 * turn) % BEAMS
     beyond = (me + BEAMS + 4 * turn) % BEAMS
     outer = (me + BEAMS - 2 * turn) % BEAMS
@@ -294,17 +293,18 @@
 
     def inward(k, send, to, slot):
         view = piece_of(rows.at[slot], k)
-        return remote(view, view, send.at[k], row_recv.at[slot, k], {"batch": to})
+        return remote(view, view, send, row_recv.at[k], {"batch": to})
 
     def across(j, k):
         return remote(
-            piece_of(row_s.at[j], k), piece_of(row_r.at[j], k), x_send.at[j, k], x_recv.at[j, k],
-            {"batch": partner},
+            piece_of(row_s.at[j], k), piece_of(row_r.at[j], k), x_send.at[0],
+            x_recv.at[j * (2 + k) + (1 - j) * (2 * k // pieces)], {"batch": partner},
         )
 
     def outward(k):
         return remote(
-            piece_of(row_s.at[2], k), piece_of(row_r.at[2], k), out_send.at[k], out_recv.at[k],
+            piece_of(row_s.at[2], k), piece_of(row_r.at[2], k), out_send.at[0],
+            out_recv.at[2 * k // pieces],
             {"batch": outer},
         )
 
@@ -316,20 +316,19 @@
         return chosen
 
     def start_inward(k):
-        inward(k, near_send, ahead, z).start()
+        inward(k, near_send.at[0], ahead, z).start()
 
         @pl.when(is_end)
         def _():
-            inward(k, far_send, beyond, z).start()
+            inward(k, far_send.at[0], beyond, z).start()
 
     def start_across(k):
         which, at = k * span // cache_len, k * span % cache_len
 
         @pl.when(is_mid)
         def _():
-            for slot in (z - turn, z + turn, z + 2 * turn):
-                slot = (slot + zs) % zs
-                inward(k, near_send, ahead, slot).wait_recv()
+            three = rows.at[pl.ds(0, zs - 1), which, pl.ds(at, span)]
+            remote(three, three, near_send.at[0], row_recv.at[k], {"batch": ahead}).wait_recv()
             for j, beam in enumerate((partner, beside)):
                 row_s[j, which, at : at + span] = row_of(beam, which, at)
                 across(j, k).start()
@@ -346,19 +345,20 @@
             )
             outward(k).start()
 
+    def whole(view, sem, to):
+        return remote(view, view, sem.at[0], sem.at[0], {"batch": to})
+
     def rows_sent():
-        for k in range(pieces):
-            inward(k, near_send, ahead, z).wait_send()
-
-            @pl.when(is_end)
-            def _():
-                inward(k, far_send, beyond, z).wait_send()
-
-            @pl.when(is_mid)
-            def _():
-                across(0, k).wait_send()
-                across(1, k).wait_send()
-                outward(k).wait_send()
+        whole(rows.at[z], near_send, ahead).wait_send()
+
+        @pl.when(is_end)
+        def _():
+            whole(rows.at[z], far_send, beyond).wait_send()
+
+        @pl.when(is_mid)
+        def _():
+            whole(row_s.at[pl.ds(0, 2)], x_send, partner).wait_send()
+            whole(row_s.at[2], out_send, outer).wait_send()
 
     def bulk(stage):
         for counts, start in ((INWARD, start_inward), (ACROSS, start_across), (OUTWARD, start_outward)):
@@ -366,27 +366,33 @@
                 start(k)
 
     def finish_rows():
-        time = lax.broadcasted_iota(jnp.int32, (span, width), 0)
-        for k in range(pieces):
-            which, at = k * span // cache_len, k * span % cache_len
-            fresh = jnp.broadcast_to(new_f[which : which + 1], (span, width))
+        time = lax.broadcasted_iota(jnp.int32, (cache_len, width), 0)
+        for which in range(2):
+            fresh = jnp.broadcast_to(new_f[which : which + 1], (cache_len, width))
 
             def put(kept):
-                cache_out[0, which, at : at + span] = jnp.where(
-                    time + at == length, fresh, kept.astype(F32)
+                cache_out[0, which] = jnp.where(
+                    time == length, fresh, kept.astype(F32)
                 ).astype(BF16)
 
             @pl.when(is_mid)
             def _():
-                across(0, k).wait_recv()
-                put(jnp.where(
-                    parent % 2 == x, row_of(me, which, at), row_r[0, which, at : at + span]
-                ))
+                view = row_r.at[0, which]
+                remote(
+                    view, view, x_recv.at[which], x_recv.at[which], {"batch": partner}
+                ).wait_recv()
+                mine = rows[0, which]
+                for index in range(1, zs):
+                    mine = jnp.where(parent // 2 == index, rows[index, which], mine)
+                put(jnp.where(parent % 2 == x, mine, row_r[0, which]))
 
             @pl.when(is_end)
             def _():
-                outward(k).wait_recv()
-                put(row_r[2, which, at : at + span])
+                view = row_r.at[2, which]
+                remote(
+                    view, view, out_recv.at[which], out_recv.at[which], {"batch": outer}
+                ).wait_recv()
+                put(row_r[2, which])
 
     locals_[8].wait()
     locals_[9].wait()
@@ -394,8 +400,7 @@
     bulk(0)
     locals_[1].wait()
     locals_[3].wait()
-    for source in sources:
-        arrived(lambda s: qall.at[s], q_recv, source)
+    all_of(lambda s: qall.at[s], q_recv.at[0]).wait_recv()
 
     length = len_ref[0]
     queries = qall[...].astype(F32)
@@ -440,7 +445,7 @@
             stats = jnp.where(lane == 2 * kind * SLOTS + h, peak[cut], stats)
             stats = jnp.where(lane == (2 * kind + 1) * SLOTS + h, total[cut], stats)
     part_s[:, heads, :] = stats
-    sent += to_peers(lambda p: part_s.at[p], lambda s: part_r.at[s], part_send, part_recv)
+    sent += to_peers(lambda p: part_s.at[p], lambda s: part_r.at[s], part_send.at[0], part_recv.at[0])
     bulk(1)
     part_r[me] = part_s[me]
 
@@ -453,8 +458,7 @@
     new_f = kv[...].astype(F32)
     new_score = jnp.sum(rows_of(own_q[0:1] * new_f[0:1]), axis=1, keepdims=True) / math.sqrt(HD)
     new_value = rows_of(new_f[1:2])
-    for source in sources:
-        arrived(lambda s: part_r.at[s], part_recv, source)
+    all_of(lambda s: part_r.at[s], part_recv.at[0]).wait_recv()
     parent = par_ref[0, me]
     turned = part_r[:, heads, :].T
     beam = lax.broadcasted_iota(jnp.int32, (LANES, BEAMS), 1)
@@ -473,12 +477,11 @@
     cross_out = numer / denom
     spare = jnp.zeros((SLOTS - heads, LANES), F32)
     att[me] = jnp.concatenate([self_out, spare, cross_out, spare], axis=0).astype(BF16)
-    sent += to_peers(lambda p: att.at[me], lambda s: att.at[s], att_send, att_recv)
+    sent += to_peers(lambda p: att.at[me], lambda s: att.at[s], att_send.at[0], att_recv.at[0])
     bulk(2)
     locals_[4].wait()
     locals_[5].wait()
-    for source in sources:
-        arrived(lambda s: att.at[s], att_recv, source)
+    all_of(lambda s: att.at[s], att_recv.at[0]).wait_recv()
     attended = att[...].astype(F32)
     for kind in range(2):
         for h in range(heads):
@@ -492,7 +495,7 @@
     hidden = (res[...].astype(F32) + (pp_s[...] + pp_r[...])).astype(BF16)
     hid_all[me] = hidden
     sent += [pair] + to_peers(
-        lambda p: hid_all.at[me], lambda s: hid_all.at[s], hid_send, hid_recv
+        lambda p: hid_all.at[me], lambda s: hid_all.at[s], hid_send.at[0], hid_recv.at[me]
     )
     hid_out[0] = hidden
     bulk(3)
@@ -544,8 +547,7 @@
             rs_s[c, :, i, :] = sums[:, i * LANES : (i + 1) * LANES]
         for peer in peers:
             remote(
-                rs_s.at[c, peer], rs_r.at[c, me], rs_send.at[c, peer], rs_recv.at[c, me],
-                {"batch": peer},
+                rs_s.at[c, peer], rs_r.at[c, me], rs_send.at[0], rs_recv.at[c], {"batch": peer}
             ).start()
         rs_r[c, me] = rs_s[c, me]
         return carry
@@ -558,11 +560,7 @@
     rows_sent()
 
     def collect_chunk(c):
-        for source in sources:
-            remote(
-                rs_r.at[c, source], rs_r.at[c, source], rs_recv.at[c, source],
-                rs_recv.at[c, source], {"batch": source},
-            ).wait_recv()
+        all_of(lambda s: rs_r.at[c, s], rs_recv.at[c]).wait_recv()
         sums = rs_r[c, 0]
         for p in range(1, BEAMS):
             sums = sums + rs_r[c, p]
@@ -572,12 +570,8 @@
 
     for c in range(chunks):
         collect_chunk(c)
-    for c in range(chunks):
-        for peer in peers:
-            remote(
-                rs_s.at[c, peer], rs_r.at[c, me], rs_send.at[c, peer], rs_recv.at[c, me],
-                {"batch": peer},
-            ).wait_send()
+    every = rs_s.at[:, pl.ds(0, BEAMS - 1)]
+    remote(every, every, rs_send.at[0], rs_send.at[0], {"batch": partner}).wait_send()
 
 
 def place_kernel(*refs):
@@ -660,25 +654,25 @@
             pltpu.VMEM((3,) + row, BF16),
             pltpu.VMEM((3,) + row, BF16),
             dma((10,)),
-            dma((BEAMS,)),
-            dma((BEAMS,)),
-            dma((BEAMS,)),
-            dma((BEAMS,)),
-            dma((BEAMS,)),
-            dma((BEAMS,)),
+            dma((1,)),
+            dma((1,)),
+            dma((1,)),
+            dma((1,)),
+            dma((1,)),
+            dma((1,)),
             dma((2,)),
             dma((2,)),
+            dma((1,)),
             dma((BEAMS,)),
-            dma((BEAMS,)),
-            dma((chunks, BEAMS)),
-            dma((chunks, BEAMS)),
+            dma((1,)),
+            dma((chunks,)),
+            dma((1,)),
+            dma((1,)),
             dma((PIECES,)),
-            dma((PIECES,)),
-            dma((BEAMS // 2, PIECES)),
-            dma((2, PIECES)),
-            dma((2, PIECES)),
-            dma((PIECES,)),
-            dma((PIECES,)),
+            dma((1,)),
+            dma((2 + PIECES,)),
+            dma((1,)),
+            dma((2,)),
             pltpu.SMEM(parents.shape, jnp.int32),
             pltpu.SMEM(lengths.shape, jnp.int32),
         ],

time: 45.3 us -> 43.7 us (0.965)
  Pallas kernels: 43.8 us -> 42.2 us
    pallas_call x1, Pallas kernels: 43 us -> 41.5 us  [kernel_body(): pl.pallas_call(step_kernel, out_shape=(pltpu.VMEM(residual.shape, BF16),...]
where the time goes in v2:
time: 43.7 us; the launch traced here: 43.5 us
  Pallas kernels  42.2 us (97%)
  between operations  1.29 us (3%)
    pallas_call x1, Pallas kernels, kernel_body(): pl.pallas_call(step_kernel, out_shape=(pltpu.VMEM(residual.shape, BF16),...  41.5 us

profile of v2, /device:TPU:0, one launch (start us, length us, event | category | flops | bytes accessed | tf_op | source)
XLA Modules:
  0.0 43.5 jit_solution(11877549484397802287)
XLA Ops:
  1.3 41.5 %shard_map.121 = (bf16[1,8,768]{2,1,0:T(8,128)(2,1)S(1)}, bf16[1,1,3072]{2,1,0:T(2,128)(2,1)S(1)}, bf16[1,2,64,1536]{3,2,1,0:T(8,128)(2,1)S(1)}) custom-call(bf16[1,1,2,1536]{3,2,1,0:T(2,128)(2,1)} %q_hbm.1, bf16[1,1,2,1536]{3,2,1,0:T(2,128)(2,1)} %kv_hbm.1, bf16[1,2,64,1536]{3,2,1,0:T(8,128)(2,1)} %cache_hbm.1, bf16[1,2,64,1536]{3,2,1,0:T(8,128)(2,1)} %mem_hbm.1, ...), custom_call_target="tpu_custom_call" | custom-call | tf_op jit(solution)/shard_map/pallas_call | solution.py:624
  42.8 0.8 %shard_map.122 = (bf16[1,8,768]{2,1,0:T(8,128)(2,1)}, bf16[1,1,3072]{2,1,0:T(2,128)(2,1)}, bf16[1,2,64,1536]{3,2,1,0:T(8,128)(2,1)}) custom-call(bf16[1,8,768]{2,1,0:T(8,128)(2,1)S(1)} %get-tuple-element.6.refs_0_, bf16[1,1,3072]{2,1,0:T(2,128)(2,1)S(1)} %get-tuple-element.7.refs_1_, bf16[1,2,64,1536]{3,2,1,0:T(8,128)(2,1)S(1)} %get-tuple-element.8.refs_2_), custom_call_target="tpu_custom_call" | custom-call | tf_op jit(solution)/shard_map/pallas_call | solution.py:593
